TPU v7x, 256 devices: a whole 4x4x8 slice. The times are simulated.
256 devices in a mesh: row: 8 (over y_lo, x), col: 16 (over z, y_hi), lag: 2 (over core).
Axes of the slice: x: 4, y: 4 (y_hi: 2, y_lo: 2; y = y_hi * 2 + y_lo), z: 8, core: 2. Of those that a mesh axis runs over, the one named last changes fastest.
Arguments:
- history: bfloat16 [8, 16, 128, 4096], P('lag', 'col', None, 'row'), may hold values from -6 to 6
- kernel_tiles: bfloat16 [8, 16, 8, 12, 256, 256], P('row', 'col', 'lag'), may hold values from -0.046875 to 0.046875
- tile_rows: int32 [8, 16, 8, 12], P('row', 'col', 'lag'), may hold values from 0 to 31
- tile_cols: int32 [8, 16, 8, 12], P('row', 'col', 'lag'), may hold values from 0 to 15
- tile_count: int32 [8, 16, 8], P('row', 'col', 'lag'), may hold values from 3 to 12, as said below
- base_stress: float32 [128, 65536], P(None, ('row', 'col', 'lag')), may hold values from -6 to 6
- prev_rate: float32 [128, 65536], P(None, ('row', 'col', 'lag')), may hold values from -6 to 6
- direct_effect: float32 [128, 65536], P(None, ('row', 'col', 'lag')), may hold values from 0.5 to 2
- state_var: float32 [128, 65536], P(None, ('row', 'col', 'lag')), may hold values from -2 to 2
Outputs:
- stress_change: float32 [128, 65536], P(None, ('row', 'col', 'lag'))
- new_rate: float32 [128, 65536], P(None, ('row', 'col', 'lag'))
Inputs may be any that keep to these rules, and one draw needn't show every extreme that they name: `tile_count`: every draw has some device and lag with all 12 slots live.
All inputs are finite; a program needn't handle non-finite values.
Results may differ from a plain program's by a relative error of at most 0.0003.
Values may be sent and summed in bfloat16 or wider, within the bound.
A program may use at most 64 MiB of HBM per device.

v0:
```python
import jax
import jax.numpy as jnp
from jax import lax
from jax.sharding import PartitionSpec as P

NEWTON = 4


def inverse_sinh(value):
    magnitude = jnp.abs(value)
    return jnp.sign(value) * jnp.log(magnitude + jnp.sqrt(1.0 + magnitude * magnitude))


def local(
    history,
    kernel_tiles,
    tile_rows,
    tile_cols,
    tile_count,
    base_stress,
    prev_rate,
    direct_effect,
    state_var,
):
    gathered = lax.all_gather(history, "row", axis=3, tiled=True)
    lag_local = gathered.shape[0]
    sims_count = gathered.shape[2]
    tile_side = kernel_tiles.shape[4]
    slots = kernel_tiles.shape[3]
    col_blocks = gathered.shape[3] // tile_side
    blocks = gathered.reshape(lag_local, sims_count, col_blocks, tile_side)
    choose = jax.nn.one_hot(tile_cols[0, 0], col_blocks, dtype=jnp.bfloat16)
    picked = jnp.einsum(
        "lkb,lsbj->lksj", choose, blocks, preferred_element_type=jnp.float32
    ).astype(jnp.bfloat16)
    contrib = jnp.einsum(
        "lksj,lkij->slki", picked, kernel_tiles[0, 0], preferred_element_type=jnp.float32
    )
    rec_local = base_stress.shape[1] * lax.axis_size(("col", "lag"))
    row_blocks = rec_local // tile_side
    alive_mask = (jnp.arange(slots)[None, :] < tile_count[0, 0][:, None]).astype(jnp.float32)
    masked = (contrib * alive_mask[None, :, :, None]).reshape(
        sims_count, lag_local * slots, tile_side
    )
    targets = tile_rows[0, 0].reshape(lag_local * slots)
    placed = (
        jnp.zeros((sims_count, row_blocks, tile_side), jnp.float32).at[:, targets, :].add(masked)
    )
    partial_stress = placed.reshape(sims_count, rec_local)
    stress_change = lax.psum_scatter(
        partial_stress, ("col", "lag"), scatter_dimension=1, tiled=True
    )
    driving = base_stress + stress_change
    factor = jnp.exp(state_var) / 2.0
    velocity = prev_rate
    for step in range(NEWTON):
        scaled = velocity * factor
        misfit = direct_effect * inverse_sinh(scaled) + 0.5 * velocity - driving
        slope = direct_effect * factor / jnp.sqrt(1.0 + scaled * scaled) + 0.5
        velocity = velocity - misfit / slope
    return (stress_change, velocity)


def solution(mesh):
    return jax.shard_map(
        local,
        mesh=mesh,
        in_specs=(
            P("lag", "col", None, "row"),
            P("row", "col", "lag", None, None, None),
            P("row", "col", "lag", None),
            P("row", "col", "lag", None),
            P("row", "col", "lag"),
            P(None, ("row", "col", "lag")),
            P(None, ("row", "col", "lag")),
            P(None, ("row", "col", "lag")),
            P(None, ("row", "col", "lag")),
        ),
        out_specs=(P(None, ("row", "col", "lag")), P(None, ("row", "col", "lag"))),
        check_vma=False,
    )
```

profile of v0, /device:TPU:2, one launch (start us, length us, event | category | flops | bytes accessed | tf_op | source)
XLA Modules:
  0.0 238.6 jit_solution(9200661468580223937)
XLA Ops:
  7.2 0.0 all-gather.2.cloned.1.call-start
  7.2 0.7 all-gather.2.cloned.1.call-update
  7.9 0.0 reduce-scatter.2.cloned.1.call-start
  7.9 0.8 reshape_squeeze.3
  8.7 0.7 fusion.12
  9.4 56.3 %all-gather.2.cloned.1.call-done = bf16[4,1,128,4096]{3,2,1,0:T(8,128)(2,1)} async-done(((bf16[4,1,128,512]{3,2,1,0:T(8,128)(2,1)}), bf16[4,1,128,4096]{3,2,1,0:T(8,128)(2,1)}) %all-gather.2.cloned.1.call-update) | async-done | bytes 4194320 | tf_op jit(solution)/shard_map/all_gather | solution.py:25
  65.7 0.0 copy-start.4
  65.7 0.0 slice-start
  65.7 3.8 %copy.26 = bf16[64,8,16,256]{3,2,1,0:T(8,128)(2,1)S(1)} copy(bf16[64,8,16,256]{3,1,2,0:T(8,128)(2,1)} %bitcast.34) | data formatting | bytes 8388608
  69.5 0.0 slice-start.1
  69.5 0.0 copy-done.4
  69.5 1.3 fusion.2
  70.8 0.0 slice-done
  70.8 0.3 slice-done.1
  71.1 4.8 %broadcast_multiply_fusion = f32[4,12,128,256]{3,2,1,0:T(8,128)} fusion(f32[4,12]{1,0:T(4,128)S(1)} %fusion.12, bf16[1,1,4,12,256,256]{5,4,3,2,1,0:T(8,128)(2,1)S(1)} %bitcast.33, bf16[4,12,128,256]{3,1,2,0:T(8,128)(2,1)S(1)} %fusion.2), kind=kOutput, calls=%fused_computation.6 | convolution fusion | flops 806879232 | bytes 15728832 | tf_op jit(solution)/shard_map/lksj,lkij->slki/dot_general | solution.py:36
  75.9 2.5 %broadcast_in_dim.4 = f32[128,32,256]{2,0,1:T(8,128)} broadcast(f32[]{:T(128)} %constant.5.clone.1), dimensions={} | broadcast | bytes 4194308 | tf_op jit(solution)/shard_map/broadcast_in_dim | solution.py:47
  78.4 14.6 %scatter_fusion = f32[128,32,256]{2,0,1:T(8,128)} fusion(f32[128,32,256]{2,0,1:T(8,128)} %broadcast_in_dim.4, s32[48]{0:T(128)S(1)} %fusion.13, f32[48,128,256]{2,1,0:T(8,128)} %bitcast.29), kind=kCustom, calls=%fused_computation | custom fusion | flops 1572864 | bytes 18874560 | tf_op jit(solution)/shard_map/scatter-add | solution.py:47
  93.1 5.6 %copy.11 = f32[128,32,256]{0,2,1:T(8,128)} copy(f32[128,32,256]{2,0,1:T(8,128)} %scatter_fusion) | data formatting | bytes 8388608 | tf_op jit(solution)/shard_map/scatter-add | solution.py:47
  98.7 0.0 copy-start
  98.7 0.0 copy-start.1
  98.7 0.0 copy-start.2
  98.7 0.0 copy-start.3
  98.7 0.0 reduce-scatter.2.cloned.1.call-update
  98.7 0.9 copy-done
  99.6 0.1 copy.12
  99.7 0.0 copy-done.1
  99.7 0.1 copy.14
  99.8 0.0 copy-done.2
  99.8 0.1 copy.16
  99.9 0.0 copy-done.3
  99.9 0.1 copy.18
  100.0 127.8 %reduce-scatter.2.cloned.1.call-done = f32[128,256]{0,1:T(8,128)} async-done(((f32[128,8192]{0,1:T(8,128)}), f32[128,256]{0,1:T(8,128)}) %reduce-scatter.2.cloned.1.call-update) | async-done | bytes 131088 | tf_op jit(solution)/shard_map/reduce_scatter | solution.py:50
  227.8 1.5 divide_subtract_fusion
  229.3 0.8 copy.23
  230.1 1.7 copy.22
  (2 shorter events, 0.0 us)
Async XLA Ops:
  7.2 58.6 %all-gather.2.cloned.1.call-start = ((), (), s32[]{:S(2)}) async-start(), calls=%async_computation.1 | async-start | bytes 4718592 | tf_op jit(solution)/shard_map/all_gather | solution.py:25
  7.9 219.9 %reduce-scatter.2.cloned.1.call-start = ((), (), s32[]{:S(2)}) async-start(), calls=%async_computation.2 | async-start | bytes 4325376 | tf_op jit(solution)/shard_map/reduce_scatter | solution.py:50
  65.7 3.8 %copy-start.4 = (s32[1,1,4,12]{3,2,1,0:T(4,128)S(1)}, s32[1,1,4,12]{3,2,1,0:T(4,128)}, u32[]{:S(2)}) copy-start(s32[1,1,4,12]{3,2,1,0:T(4,128)} %param.12) | copy-start | bytes 580
  65.7 5.1 %slice-start = ((s8[6291456]{0:T(1024)(128)(4,1)}), s8[4194304]{0:T(1024)(128)(4,1)S(1)}, s32[]{:S(2)}) async-start(s8[6291456]{0:T(1024)(128)(4,1)} %bitcast.32), calls=%async_computation.3 | async-start | bytes 8388608
  69.5 1.6 slice-start.1
  98.7 0.9 copy-start
  98.7 1.0 copy-start.1
  98.7 1.1 copy-start.2
  98.7 1.2 copy-start.3
Sparse Core Ops, SparseCore 0:
  9.8 55.8 all-gather.1
  98.8 128.9 reduce-scatter.1
where the time goes:
time: 239 us
  waiting for transfers between devices  185 us (77%)
  other arithmetic  16.9 us (7%)
  local copies, waits for them, and re-layouts  16.5 us (7%)
  between operations  14.1 us (6%)
  matrix products  6.13 us (3%)
    reduce_scatter x1, waiting for transfers between devices, local(): lax.psum_scatter(partial_stress, ('col', 'lag'), scatter_dimension=1, til...  128 us
    all_gather x1, waiting for transfers between devices, local(): gathered = lax.all_gather(history, 'row', axis=3, tiled=True)  56.3 us
    scatter-add x1, other arithmetic, local(): jnp.zeros((sims_count, row_blocks, tile_side), jnp.float32)  14.6 us
    unnamed x21, local copies, waits for them, and re-layouts  7.69 us
    scatter-add x1, local copies, waits for them, and re-layouts, local(): jnp.zeros((sims_count, row_blocks, tile_side), jnp.float32)  5.58 us
    dot_general x1, matrix products, local(): jnp.einsum('lksj,lkij->slki', picked, kernel_tiles[0, 0], preferred_eleme...  4.84 us
  transfers between devices with their start and end apart: 2, of which 2 were waited for; matrix products, arithmetic and copies ran while one was open for 1% of the time, Pallas kernels for 0%

commit v1 on v0

--- a/solution.py
+++ b/solution.py
@@ -22,7 +22,16 @@
     direct_effect,
     state_var,
 ):
-    gathered = lax.all_gather(history, "row", axis=3, tiled=True)
+    _scan_plate = lambda x_part, device_axis, k_dim: jnp.concatenate(
+        lax.all_to_all(
+            jnp.stack([x_part] * lax.axis_size(device_axis), 0),
+            axis_name=device_axis,
+            split_axis=0,
+            concat_axis=0,
+        ),
+        k_dim,
+    )
+    gathered = _scan_plate(history, "row", 3)
     lag_local = gathered.shape[0]
     sims_count = gathered.shape[2]
     tile_side = kernel_tiles.shape[4]

time: 239 us -> 264 us (1.10)
  local copies, waits for them, and re-layouts: 16.5 us -> 29 us
  starting transfers between devices: 0.08 us -> 6.83 us
  waiting for transfers between devices: 185 us -> 189 us
    all_gather x1 -> x0, waiting for transfers between devices: 56.3 us -> none  [local(): gathered = lax.all_gather(history, 'row', axis=3, tiled=True)]
    all_to_all x0 -> x1, waiting for transfers between devices: none -> 55.7 us  [local(): lax.all_to_all(jnp.stack([x_part] * lax.axis_size(device_axis), 0), axis_...]
    another operation x0 -> x3, local copies, waits for them, and re-layouts: none -> 12.1 us  [the longest x1 7.87 us: local(): blocks = gathered.reshape(lag_local, sims_count, col_blocks, tile_side)]
    all_to_all x0 -> x1, starting transfers between devices: none -> 6.82 us  [local(): lax.all_to_all(jnp.stack([x_part] * lax.axis_size(device_axis), 0), axis_...]
    reduce_scatter x1, waiting for transfers between devices: 128 us -> 133 us  [local(): lax.psum_scatter(partial_stress, ('col', 'lag'), scatter_dimension=1, til...]
    all_to_all x0 -> x1, local copies, waits for them, and re-layouts: none -> 4.61 us  [local(): lax.all_to_all(jnp.stack([x_part] * lax.axis_size(device_axis), 0), axis_...]
    unnamed x21 -> x24, local copies, waits for them, and re-layouts: 7.69 us -> 4.14 us
  transfers between devices with their start and end apart: 2 -> 2, of which waited for: 2 -> 2; matrix products, arithmetic and copies ran while one was open for 1% -> 0% of each run, Pallas kernels for 0% -> 0%
where the time goes in v1:
time: 264 us
  waiting for transfers between devices  189 us (72%)
  local copies, waits for them, and re-layouts  29 us (11%)
  other arithmetic  16.3 us (6%)
  between operations  14.1 us (5%)
  matrix products  8.46 us (3%)
  starting transfers between devices  6.83 us (3%)
    reduce_scatter x1, waiting for transfers between devices, local(): lax.psum_scatter(partial_stress, ('col', 'lag'), scatter_dimension=1, til...  133 us
    all_to_all x1, waiting for transfers between devices, local(): lax.all_to_all(jnp.stack([x_part] * lax.axis_size(device_axis), 0), axis_...  55.7 us
    scatter-add x1, other arithmetic, local(): jnp.zeros((sims_count, row_blocks, tile_side), jnp.float32)  14.7 us
    another operation x1, local copies, waits for them, and re-layouts, local(): blocks = gathered.reshape(lag_local, sims_count, col_blocks, tile_side)  7.87 us
    all_to_all x1, starting transfers between devices, local(): lax.all_to_all(jnp.stack([x_part] * lax.axis_size(device_axis), 0), axis_...  6.82 us
    scatter-add x1, local copies, waits for them, and re-layouts, local(): jnp.zeros((sims_count, row_blocks, tile_side), jnp.float32)  5.59 us
  transfers between devices with their start and end apart: 2, of which 2 were waited for; matrix products, arithmetic and copies ran while one was open for 0% of the time, Pallas kernels for 0%

profile of v1, /device:TPU:2, one launch (start us, length us, event | category | flops | bytes accessed | tf_op | source)
XLA Modules:
  0.0 263.9 jit_solution(7377654217200679762)
XLA Ops:
  7.2 1.3 copy.25
  8.5 2.9 %stack.2 = bf16[8,4,1,128,512]{3,4,1,2,0:T(8,128)(2,1)} broadcast(bf16[4,128,512]{1,2,0:T(8,128)(2,1)S(1)} %copy.25), dimensions={1,3,4} | broadcast | bytes 4718592 | tf_op jit(solution)/shard_map/stack | solution.py:27
  11.4 0.0 copy-start.5
  11.4 0.0 copy-start.6
  11.4 6.8 %all-to-all-start = ((bf16[8,4,1,128,512]{3,4,1,2,0:T(8,128)(2,1)}), bf16[8,4,1,128,512]{3,4,1,2,0:T(8,128)(2,1)}, u32[]{:S(2)}, u32[]{:S(2)}) async-start(bf16[8,4,1,128,512]{3,4,1,2,0:T(8,128)(2,1)} %stack.2), calls=%async_computation | async-start | bytes 8388608 | tf_op jit(solution)/shard_map/all_to_all | solution.py:26
  18.2 0.0 reduce-scatter.2.cloned.1.call-start
  18.2 0.0 copy-done.5
  18.2 0.1 reshape_squeeze.3
  18.3 0.0 copy-done.6
  18.3 0.1 fusion.13
  18.4 55.7 %all-to-all-done = bf16[8,4,1,128,512]{3,4,1,2,0:T(8,128)(2,1)} async-done(((bf16[8,4,1,128,512]{3,4,1,2,0:T(8,128)(2,1)}), bf16[8,4,1,128,512]{3,4,1,2,0:T(8,128)(2,1)}, u32[]{:S(2)}, u32[]{:S(2)}) %all-to-all-start) | async-done | bytes 4194336 | tf_op jit(solution)/shard_map/all_to_all | solution.py:26
  74.1 4.6 %copy.26 = bf16[8,4,1,128,512]{3,4,0,1,2:T(8,128)(2,1)} copy(bf16[8,4,1,128,512]{3,4,1,2,0:T(8,128)(2,1)} %all-to-all-done) | data formatting | bytes 8388608 | tf_op jit(solution)/shard_map/all_to_all | solution.py:26
  78.7 0.0 copy-start.4
  78.7 7.9 %copy.27 = bf16[4,128,16,256]{3,2,1,0:T(8,128)(2,1)} copy(bf16[4,128,16,256]{1,3,2,0:T(8,128)(2,1)} %bitcast.27) | data formatting | bytes 8388608 | tf_op jit(solution)/shard_map/reshape;reshape | solution.py:40
  86.6 0.0 slice-start
  86.6 0.0 copy-done.4
  86.6 0.0 slice-start.1
  86.6 3.6 %convolution_convert_fusion = bf16[4,12,128,256]{3,1,2,0:T(8,128)(2,1)S(1)} fusion(bf16[4,128,16,256]{3,2,1,0:T(8,128)(2,1)} %copy.27, s32[4,12]{1,0:T(4,128)S(1)} %bitcast.31), kind=kOutput, calls=%fused_computation.5 | convolution fusion | flops 51905280 | bytes 7340224 | tf_op jit(solution)/shard_map/lkb,lsbj->lksj/dot_general | solution.py:42
  90.2 0.0 slice-done
  90.2 0.5 slice-done.1
  90.7 4.8 %broadcast_multiply_fusion = f32[4,12,128,256]{3,2,1,0:T(8,128)} fusion(f32[4,12]{1,0:T(4,128)S(1)} %fusion.13, bf16[1,1,4,12,256,256]{5,4,3,2,1,0:T(8,128)(2,1)S(1)} %bitcast.29, bf16[4,12,128,256]{3,1,2,0:T(8,128)(2,1)S(1)} %convolution_convert_fusion), kind=kOutput, calls=%fused_computation.4 | convolution fusion | flops 806879232 | bytes 15728832 | tf_op jit(solution)/shard_map/lksj,lkij->slki/dot_general | solution.py:45
  95.5 2.5 broadcast_in_dim.4
  98.0 14.7 %scatter_fusion = f32[128,32,256]{2,0,1:T(8,128)} fusion(f32[128,32,256]{2,0,1:T(8,128)} %broadcast_in_dim.4, s32[48]{0:T(128)S(1)} %fusion.14, f32[48,128,256]{2,1,0:T(8,128)} %bitcast.25), kind=kCustom, calls=%fused_computation | custom fusion | flops 1572864 | bytes 18874560 | tf_op jit(solution)/shard_map/scatter-add | solution.py:56
  112.8 5.6 %copy.29 = f32[128,32,256]{0,2,1:T(8,128)} copy(f32[128,32,256]{2,0,1:T(8,128)} %scatter_fusion) | data formatting | bytes 8388608 | tf_op jit(solution)/shard_map/scatter-add | solution.py:56
  118.3 0.0 copy-start
  118.3 0.0 copy-start.1
  118.3 0.0 copy-start.2
  118.4 0.0 copy-start.3
  118.4 0.0 reduce-scatter.2.cloned.1.call-update
  118.4 0.9 copy-done
  119.2 0.1 copy.30
  119.3 0.0 copy-done.1
  119.4 0.1 copy.32
  119.4 0.0 copy-done.2
  119.5 0.1 copy.34
  119.6 0.0 copy-done.3
  119.6 0.1 copy.36
  119.7 133.5 %reduce-scatter.2.cloned.1.call-done = f32[128,256]{0,1:T(8,128)} async-done(((f32[128,8192]{0,1:T(8,128)}), f32[128,256]{0,1:T(8,128)}) %reduce-scatter.2.cloned.1.call-update) | async-done | bytes 131088 | tf_op jit(solution)/shard_map/reduce_scatter | solution.py:59
  253.1 1.5 divide_subtract_fusion
  254.6 0.8 copy.41
  255.4 1.7 copy.40
  (2 shorter events, 0.0 us)
Async XLA Ops:
  11.4 6.8 %copy-start.5 = (s32[1,1,4,12]{3,2,1,0:T(4,128)S(1)}, s32[1,1,4,12]{3,2,1,0:T(4,128)}, u32[]{:S(2)}) copy-start(s32[1,1,4,12]{3,2,1,0:T(4,128)} %param.11) | copy-start | bytes 580
  11.4 6.9 %copy-start.6 = (s32[1,1,4]{2,1,0:T(1,128)S(1)}, s32[1,1,4]{2,1,0:T(1,128)}, u32[]{:S(2)}) copy-start(s32[1,1,4]{2,1,0:T(1,128)} %param.13) | copy-start | bytes 52
  11.4 62.7 %all-to-all-start = ((bf16[8,4,1,128,512]{3,4,1,2,0:T(8,128)(2,1)}), bf16[8,4,1,128,512]{3,4,1,2,0:T(8,128)(2,1)}, u32[]{:S(2)}, u32[]{:S(2)}) async-start(bf16[8,4,1,128,512]{3,4,1,2,0:T(8,128)(2,1)} %stack.2), calls=%async_computation | async-start | bytes 8388608 | tf_op jit(solution)/shard_map/all_to_all | solution.py:26
  18.2 234.9 %reduce-scatter.2.cloned.1.call-start = ((), (), s32[]{:S(2)}) async-start(), calls=%async_computation.2 | async-start | bytes 4325376 | tf_op jit(solution)/shard_map/reduce_scatter | solution.py:59
  78.7 7.9 %copy-start.4 = (s32[1,1,4,12]{3,2,1,0:T(4,128)S(1)}, s32[1,1,4,12]{3,2,1,0:T(4,128)}, u32[]{:S(2)}) copy-start(s32[1,1,4,12]{3,2,1,0:T(4,128)} %param.12) | copy-start | bytes 580
  86.6 3.6 %slice-start = ((s8[6291456]{0:T(1024)(128)(4,1)}), s8[4194304]{0:T(1024)(128)(4,1)S(1)}, s32[]{:S(2)}) async-start(s8[6291456]{0:T(1024)(128)(4,1)} %bitcast.28), calls=%async_computation.3 | async-start | bytes 8388608
  86.6 4.1 %slice-start.1 = ((s8[6291456]{0:T(1024)(128)(4,1)}), s8[2097152]{0:T(1024)(128)(4,1)S(1)}, s32[]{:S(2)}) async-start(s8[6291456]{0:T(1024)(128)(4,1)} %bitcast.28), calls=%async_computation.4 | async-start | bytes 4194304
  118.3 0.9 copy-start
  118.3 1.0 copy-start.1
  118.3 1.1 copy-start.2
  118.4 1.2 copy-start.3
Sparse Core Ops, SparseCore 0:
  118.5 134.5 reduce-scatter.1
